TPU v7x, 32 devices: a whole 2x2x4 slice. The times are simulated.
32 devices in a mesh: cand: 4 (over y, core), hid: 8 (over z, x).
Axes of the slice: x: 2, y: 2, z: 4, core: 2. Of those that a mesh axis runs over, the one named last changes fastest.
Arguments:
- tokens: bfloat16 [4, 256, 2048], P('cand', None, 'hid'), may hold values from -6 to 6
- cotangent: bfloat16 [4, 256, 2048], P('cand', None, 'hid'), may hold values from -6 to 6
- gate_weight: bfloat16 [2048, 8192], P('cand', 'hid'), may hold values from -0.125 to 0.125
- up_weight: bfloat16 [2048, 8192], P('cand', 'hid'), may hold values from -0.125 to 0.125
- down_weight: bfloat16 [8192, 2048], P('hid', 'cand'), may hold values from -0.125 to 0.125
- width_steps: int32 [4], P('cand'), may hold values from 1 to 8
- block_order: int32 [8], replicated, may hold values from 0 to 7, each once
Outputs:
- grad_tokens: float32 [4, 256, 2048], P('cand', None, 'hid')
- grad_gate: float32 [2048, 8192], P('cand', 'hid')
- grad_up: float32 [2048, 8192], P('cand', 'hid')
- grad_down: float32 [8192, 2048], P('hid', 'cand')
Inputs may be any that keep to these rules, and one draw needn't show every extreme that they name: Candidate c uses the first width_steps[c] * 1024 logical hidden units. `block_order`: names each of the 8 logical blocks once.
All inputs are finite; a program needn't handle non-finite values.
Results may differ from a plain program's by a relative error of at most 0.02.
Values may be sent and summed in bfloat16 or wider, within the bound.
A program may use at most 64 MiB of HBM per device.

v0:
```python
import jax
import jax.numpy as jnp
from jax import lax
from jax.sharding import PartitionSpec as P

FF = 8192


def shards(tokens, cotangent, gate_weight, up_weight, down_weight, width_steps, block_order):
    inputs, upstream = (
        lax.all_gather(tokens, "hid", axis=2, tiled=True),
        lax.all_gather(cotangent, "hid", axis=2, tiled=True),
    )
    inputs = inputs[0]
    upstream = upstream[0]
    gate_full, up_full = (
        lax.all_gather(gate_weight, "cand", axis=0, tiled=True),
        lax.all_gather(up_weight, "cand", axis=0, tiled=True),
    )
    down_full = lax.all_gather(down_weight, "cand", axis=1, tiled=True)
    width = gate_weight.shape[1]
    places = jnp.arange(block_order.shape[0], dtype=jnp.int32)
    logical = jnp.sum(jnp.where(places == lax.axis_index("hid"), block_order, 0))
    active = logical * width < width_steps[0] * (FF // 8)
    keep = active.astype(jnp.float32)
    gate = jnp.dot(inputs, gate_full, preferred_element_type=jnp.float32)
    up = jnp.dot(inputs, up_full, preferred_element_type=jnp.float32)
    sig = jax.nn.sigmoid(gate)
    act = keep * gate * sig
    hidden = (act * up).astype(jnp.bfloat16)
    dhid = keep * jnp.einsum("td,fd->tf", upstream, down_full, preferred_element_type=jnp.float32)
    forward_d_up = (dhid * act).astype(jnp.bfloat16)
    forward_d_gate = (dhid * up * keep * sig * (1.0 + gate * (1.0 - sig))).astype(jnp.bfloat16)
    down_local = jnp.einsum("tf,td->fd", hidden, upstream, preferred_element_type=jnp.float32)
    down_local, d_gate, d_up = (down_local, forward_d_gate, forward_d_up)
    gate_local = jnp.einsum("td,tf->df", inputs, d_gate, preferred_element_type=jnp.float32)
    up_local = jnp.einsum("td,tf->df", inputs, d_up, preferred_element_type=jnp.float32)
    input_part = jnp.einsum("tf,df->td", d_gate, gate_full, preferred_element_type=jnp.float32)
    input_part = input_part + jnp.einsum(
        "tf,df->td", d_up, up_full, preferred_element_type=jnp.float32
    )
    gate_local, up_local, input_part = (gate_local, up_local, input_part)
    grad_tokens = lax.psum_scatter(
        input_part[None].astype(jnp.bfloat16), "hid", scatter_dimension=2, tiled=True
    ).astype(jnp.float32)
    grad_gate, grad_up = (
        lax.psum_scatter(
            gate_local.astype(jnp.bfloat16), "cand", scatter_dimension=0, tiled=True
        ).astype(jnp.float32),
        lax.psum_scatter(
            up_local.astype(jnp.bfloat16), "cand", scatter_dimension=0, tiled=True
        ).astype(jnp.float32),
    )
    grad_down = lax.psum_scatter(
        down_local.astype(jnp.bfloat16), "cand", scatter_dimension=1, tiled=True
    ).astype(jnp.float32)
    return (grad_tokens, grad_gate, grad_up, grad_down)


def solution(mesh):
    in_specs = (
        P("cand", None, "hid"),
        P("cand", None, "hid"),
        P("cand", "hid"),
        P("cand", "hid"),
        P("hid", "cand"),
        P("cand"),
        P(),
    )
    out_specs = (P("cand", None, "hid"), P("cand", "hid"), P("cand", "hid"), P("hid", "cand"))
    return jax.shard_map(shards, mesh=mesh, in_specs=in_specs, out_specs=out_specs, check_vma=False)
```

profile of v0, /device:TPU:0, one launch (start us, length us, event | category | flops | bytes accessed | tf_op | source)
XLA Modules:
  0.0 422.3 jit_solution(7583610765798703201)
XLA Ops:
  7.2 0.7 all-gather.10.cloned.1.call-update
  7.9 0.7 all-gather.12.cloned.1.call-update
  8.7 0.7 all-gather.14.cloned.1.call-update
  9.4 0.5 all-gather.6.cloned.1.call-update
  10.0 0.5 all-gather.8.cloned.1.call-update
  10.5 0.0 reduce-scatter.5.cloned.1.call-start
  11.2 1.3 fusion.10
  13.2 39.0 %all-gather.10.cloned.1.call-done = bf16[1,256,2048]{2,1,0:T(8,128)(2,1)} async-done(((bf16[1,256,256]{2,1,0:T(8,128)(2,1)}), bf16[1,256,2048]{2,1,0:T(8,128)(2,1)}) %all-gather.10.cloned.1.call-update) | async-done | bytes 1048592 | tf_op jit(solution)/shard_map/all_gather | solution.py:11
  52.2 35.1 %all-gather.12.cloned.1.call-done = bf16[2048,1024]{1,0:T(8,128)(2,1)} async-done(((bf16[512,1024]{1,0:T(8,128)(2,1)}), bf16[2048,1024]{1,0:T(8,128)(2,1)}) %all-gather.12.cloned.1.call-update) | async-done | bytes 4194320 | tf_op jit(solution)/shard_map/all_gather | solution.py:18
  87.2 3.8 fusion.6
  91.0 32.3 %all-gather.14.cloned.1.call-done = bf16[2048,1024]{1,0:T(8,128)(2,1)} async-done(((bf16[512,1024]{1,0:T(8,128)(2,1)}), bf16[2048,1024]{1,0:T(8,128)(2,1)}) %all-gather.14.cloned.1.call-update) | async-done | bytes 4194320 | tf_op jit(solution)/shard_map/all_gather | solution.py:17
  123.3 4.4 %fusion.4 = f32[256,1024]{1,0:T(8,128)} fusion(bf16[2048,1024]{1,0:T(8,128)(2,1)} %all-gather.14.cloned.1.call-done, bf16[1,256,2048]{2,1,0:T(8,128)(2,1)S(1)} %copy-done), kind=kOutput, calls=%fused_computation.9 | convolution fusion | flops 1073741824 | bytes 6291456 | tf_op jit(solution)/shard_map/dot_general | solution.py:26
  127.7 36.9 %all-gather.6.cloned.1.call-done = bf16[1,256,2048]{2,1,0:T(8,128)(2,1)} async-done(((bf16[1,256,256]{2,1,0:T(8,128)(2,1)}), bf16[1,256,2048]{2,1,0:T(8,128)(2,1)}) %all-gather.6.cloned.1.call-update) | async-done | bytes 1048592 | tf_op jit(solution)/shard_map/all_gather | solution.py:12
  164.6 34.9 %all-gather.8.cloned.1.call-done = bf16[1024,2048]{1,0:T(8,128)(2,1)} async-done(((bf16[1024,512]{1,0:T(8,128)(2,1)}), bf16[1024,2048]{1,0:T(8,128)(2,1)}) %all-gather.8.cloned.1.call-update) | async-done | bytes 4194320 | tf_op jit(solution)/shard_map/all_gather | solution.py:20
  199.5 4.6 %multiply_convert_fusion.1 = (bf16[256,1024]{1,0:T(8,128)(2,1)S(1)}, bf16[256,1024]{1,0:T(8,128)(2,1)S(1)}) fusion(f32[256,1024]{1,0:T(8,128)} %fusion.4, f32[]{:T(128)S(6)} %convert_element_type.45, f32[256,1024]{1,0:T(8,128)S(1)} %fusion.6, bf16[1024,2048]{1,0:T(8,128)(2,1)} %all-gather.8.cloned.1.call-done, ...), kind=kOutput, calls=%fused_computation.16 | convolution fusion | flops 1077936128 | bytes 8388612 | tf_op jit(solution)/shard_map/td,fd->tf/dot_general | solution.py:31
  204.2 1.3 fusion.12
  205.4 0.9 copy-done.1
  206.3 2.3 fusion.1
  208.6 0.0 reduce-scatter.11.cloned.1.call-start
  208.7 4.9 %convolution_convert_fusion = bf16[1024,2048]{1,0:T(8,128)(2,1)} fusion(bf16[1,256,2048]{2,1,0:T(8,128)(2,1)S(1)} %copy-done.3, f32[256,1024]{1,0:T(8,128)} %copy-done.4, f32[256,1024]{1,0:T(8,128)} %fusion.4, f32[]{:T(128)S(6)} %convert_element_type.45), kind=kOutput, calls=%fused_computation.2 | convolution fusion | flops 1077673984 | bytes 7340036 | tf_op jit(solution)/shard_map/tf,td->fd/dot_general | solution.py:34
  213.6 0.0 reduce-scatter.9.cloned.1.call-start
  213.6 3.3 convert_bitcast_fusion
  216.9 0.0 reduce-scatter.7.cloned.1.call-start
  217.0 3.3 convert_bitcast_fusion.1
  220.2 53.1 %reduce-scatter.5.cloned.1.call-done = bf16[1,256,256]{2,1,0:T(8,128)(2,1)} async-done(((bf16[1,256,2048]{2,1,0:T(8,128)(2,1)}), bf16[1,256,256]{2,1,0:T(8,128)(2,1)}) %reduce-scatter.5.cloned.1.call-update) | async-done | bytes 131088 | tf_op jit(solution)/shard_map/reduce_scatter | solution.py:43
  273.3 1.6 convert_element_type.50
  275.0 44.3 %reduce-scatter.11.cloned.1.call-done = bf16[1024,512]{1,0:T(8,128)(2,1)} async-done(((bf16[1024,2048]{1,0:T(8,128)(2,1)}), bf16[1024,512]{1,0:T(8,128)(2,1)}) %reduce-scatter.11.cloned.1.call-update) | async-done | bytes 1048592 | tf_op jit(solution)/shard_map/reduce_scatter | solution.py:54
  319.2 2.8 convert_element_type.59
  322.1 44.1 %reduce-scatter.9.cloned.1.call-done = bf16[512,1024]{0,1:T(8,128)(2,1)} async-done(((bf16[2048,1024]{0,1:T(8,128)(2,1)}), bf16[512,1024]{0,1:T(8,128)(2,1)}) %reduce-scatter.9.cloned.1.call-update) | async-done | bytes 1048592 | tf_op jit(solution)/shard_map/reduce_scatter | solution.py:50
  366.2 2.6 copy.12
  368.8 44.4 %reduce-scatter.7.cloned.1.call-done = bf16[512,1024]{0,1:T(8,128)(2,1)} async-done(((bf16[2048,1024]{0,1:T(8,128)(2,1)}), bf16[512,1024]{0,1:T(8,128)(2,1)}) %reduce-scatter.7.cloned.1.call-update) | async-done | bytes 1048592 | tf_op jit(solution)/shard_map/reduce_scatter | solution.py:47
  413.2 2.6 copy.11
  (18 shorter events, 0.3 us)
Async XLA Ops:
  7.2 45.0 %all-gather.10.cloned.1.call-start = ((), (), s32[]{:S(2)}) async-start(), calls=%async_computation.6 | async-start | bytes 1179648 | tf_op jit(solution)/shard_map/all_gather | solution.py:11
  7.9 79.3 %all-gather.12.cloned.1.call-start = ((), (), s32[]{:S(2)}) async-start(), calls=%async_computation.7 | async-start | bytes 5242880 | tf_op jit(solution)/shard_map/all_gather | solution.py:18
  8.6 114.6 %all-gather.14.cloned.1.call-start = ((), (), s32[]{:S(2)}) async-start(), calls=%async_computation.8 | async-start | bytes 5242880 | tf_op jit(solution)/shard_map/all_gather | solution.py:17
  9.4 155.2 %all-gather.6.cloned.1.call-start = ((), (), s32[]{:S(2)}) async-start(), calls=%async_computation.4 | async-start | bytes 1179648 | tf_op jit(solution)/shard_map/all_gather | solution.py:12
  10.0 189.6 %all-gather.8.cloned.1.call-start = ((), (), s32[]{:S(2)}) async-start(), calls=%async_computation.5 | async-start | bytes 5242880 | tf_op jit(solution)/shard_map/all_gather | solution.py:20
  10.5 262.8 %reduce-scatter.5.cloned.1.call-start = ((), (), s32[]{:S(2)}) async-start(), calls=%async_computation.9 | async-start | bytes 1179648 | tf_op jit(solution)/shard_map/reduce_scatter | solution.py:43
  52.2 71.1 %copy-start = (bf16[1,256,2048]{2,1,0:T(8,128)(2,1)S(1)}, bf16[1,256,2048]{2,1,0:T(8,128)(2,1)}, u32[]{:S(2)}) copy-start(bf16[1,256,2048]{2,1,0:T(8,128)(2,1)} %all-gather.10.cloned.1.call-done) | copy-start | bytes 3145732
  91.0 113.1 %copy-start.4 = (f32[256,1024]{1,0:T(8,128)}, f32[256,1024]{1,0:T(8,128)S(1)}, u32[]{:S(2)}) copy-start(f32[256,1024]{1,0:T(8,128)S(1)} %fusion.6) | copy-start | bytes 3145732
  199.5 4.6 %copy-start.2 = (bf16[2048,1024]{1,0:T(8,128)(2,1)S(1)}, bf16[2048,1024]{1,0:T(8,128)(2,1)}, u32[]{:S(2)}) copy-start(bf16[2048,1024]{1,0:T(8,128)(2,1)} %all-gather.14.cloned.1.call-done) | copy-start | bytes 12582916
  204.1 2.2 copy-start.1
  206.3 2.3 copy-start.3
  208.6 110.6 %reduce-scatter.11.cloned.1.call-start = ((), (), s32[]{:S(2)}) async-start(), calls=%async_computation.12 | async-start | bytes 5242880 | tf_op jit(solution)/shard_map/reduce_scatter | solution.py:54
  213.6 152.6 %reduce-scatter.9.cloned.1.call-start = ((), (), s32[]{:S(2)}) async-start(), calls=%async_computation.11 | async-start | bytes 5242880 | tf_op jit(solution)/shard_map/reduce_scatter | solution.py:50
  216.9 196.3 %reduce-scatter.7.cloned.1.call-start = ((), (), s32[]{:S(2)}) async-start(), calls=%async_computation.10 | async-start | bytes 5242880 | tf_op jit(solution)/shard_map/reduce_scatter | solution.py:47
Sparse Core Ops, SparseCore 0:
  10.0 42.1 all-gather.9
  53.7 33.4 all-gather.11
  88.8 34.4 all-gather.13
  125.2 39.3 all-gather.5
  166.0 33.4 all-gather.7
  208.7 64.5 reduce-scatter.4
  275.9 43.3 reduce-scatter.10
  321.8 44.3 reduce-scatter.8
  368.7 44.3 reduce-scatter.6
where the time goes:
time: 423 us; the launch traced here: 422 us
  waiting for transfers between devices  367 us (87%)
  matrix products  27.7 us (7%)
  between operations  15.2 us (4%)
  local copies, waits for them, and re-layouts  6.02 us (1%)
  other arithmetic  5.75 us (1%)
    reduce_scatter x1, waiting for transfers between devices, shards(): lax.psum_scatter(input_part[None].astype(jnp.bfloat16), 'hid', scatter_di...  53.1 us
    reduce_scatter x1, waiting for transfers between devices, shards(): lax.psum_scatter(gate_local.astype(jnp.bfloat16), 'cand', scatter_dimensi...  44.4 us
    reduce_scatter x1, waiting for transfers between devices, shards(): lax.psum_scatter(down_local.astype(jnp.bfloat16), 'cand', scatter_dimensi...  44.3 us
    reduce_scatter x1, waiting for transfers between devices, shards(): lax.psum_scatter(up_local.astype(jnp.bfloat16), 'cand', scatter_dimension...  44.1 us
    all_gather x1, waiting for transfers between devices, shards(): lax.all_gather(tokens, 'hid', axis=2, tiled=True)  39 us
    all_gather x1, waiting for transfers between devices, shards(): lax.all_gather(cotangent, 'hid', axis=2, tiled=True)  36.9 us
    all_gather x1, waiting for transfers between devices, shards(): lax.all_gather(up_weight, 'cand', axis=0, tiled=True)  35.1 us
    all_gather x1, waiting for transfers between devices, shards(): down_full = lax.all_gather(down_weight, 'cand', axis=1, tiled=True)  34.9 us
  transfers between devices with their start and end apart: 9, of which 9 were waited for; matrix products, arithmetic and copies ran while one was open for 7% of the time, Pallas kernels for 0%

commit v1 on v0

--- a/solution.py
+++ b/solution.py
@@ -1,9 +1,26 @@
+import functools
 import jax
 import jax.numpy as jnp
 from jax import lax
 from jax.sharding import PartitionSpec as P
 
 FF = 8192
+
+
+def enter_the_heaps(here_x, mesh_name):
+    chips = lax.axis_size(mesh_name)
+    reply = [None] * chips
+    reply[chips - 1] = here_x
+    arrivals = [(tick, (tick + 1) % chips) for tick in range(chips)]
+    for dev_i in range(chips - 2, -1, -1):
+        reply[dev_i] = lax.ppermute(reply[dev_i + 1], mesh_name, arrivals)
+    v_now = jnp.concatenate(reply, 1)
+    big = lax.axis_index(mesh_name)
+    y_new = jnp.roll(v_now, (big + 1) * here_x.shape[1], 1)
+    return y_new
+
+
+refer_the_set = functools.partial(enter_the_heaps, mesh_name="cand")
 
 
 def shards(tokens, cotangent, gate_weight, up_weight, down_weight, width_steps, block_order):
@@ -17,7 +34,7 @@
         lax.all_gather(gate_weight, "cand", axis=0, tiled=True),
         lax.all_gather(up_weight, "cand", axis=0, tiled=True),
     )
-    down_full = lax.all_gather(down_weight, "cand", axis=1, tiled=True)
+    down_full = refer_the_set(down_weight)
     width = gate_weight.shape[1]
     places = jnp.arange(block_order.shape[0], dtype=jnp.int32)
     logical = jnp.sum(jnp.where(places == lax.axis_index("hid"), block_order, 0))

time: 423 us -> 387 us (0.915)
  waiting for transfers between devices: 367 us -> 318 us
  local copies, waits for them, and re-layouts: 6.02 us -> 18.7 us
    ppermute x0 -> x3, waiting for transfers between devices: none -> 40.4 us  [enter_the_heaps(): reply[dev_i] = lax.ppermute(reply[dev_i + 1], mesh_name, arrivals)]
    all_gather x1, waiting for transfers between devices: 39 us -> 0.01 us  [shards(): lax.all_gather(tokens, 'hid', axis=2, tiled=True)]
    all_gather x1 -> x0, waiting for transfers between devices: 34.9 us -> none  [shards(): down_full = lax.all_gather(down_weight, 'cand', axis=1, tiled=True)]
    unnamed x12 -> x23, local copies, waits for them, and re-layouts: 6.02 us -> 17.5 us
    all_gather x1, waiting for transfers between devices: 32.3 us -> 22.5 us  [shards(): lax.all_gather(gate_weight, 'cand', axis=0, tiled=True)]
  transfers between devices with their start and end apart: 9 -> 11, of which waited for: 9 -> 10; matrix products, arithmetic and copies ran while one was open for 7% -> 10% of each run, Pallas kernels for 0% -> 0%
where the time goes in v1:
time: 387 us
  waiting for transfers between devices  318 us (82%)
  matrix products  28.2 us (7%)
  local copies, waits for them, and re-layouts  18.7 us (5%)
  between operations  15.6 us (4%)
  other arithmetic  5.75 us (1%)
    reduce_scatter x1, waiting for transfers between devices, shards(): lax.psum_scatter(input_part[None].astype(jnp.bfloat16), 'hid', scatter_di...  51.4 us
    reduce_scatter x1, waiting for transfers between devices, shards(): lax.psum_scatter(up_local.astype(jnp.bfloat16), 'cand', scatter_dimension...  44.4 us
    reduce_scatter x1, waiting for transfers between devices, shards(): lax.psum_scatter(down_local.astype(jnp.bfloat16), 'cand', scatter_dimensi...  44.4 us
    reduce_scatter x1, waiting for transfers between devices, shards(): lax.psum_scatter(gate_local.astype(jnp.bfloat16), 'cand', scatter_dimensi...  44.2 us
    ppermute x3, waiting for transfers between devices, enter_the_heaps(): reply[dev_i] = lax.ppermute(reply[dev_i + 1], mesh_name, arrivals)  40.4 us
    all_gather x1, waiting for transfers between devices, shards(): lax.all_gather(cotangent, 'hid', axis=2, tiled=True)  36.4 us
    all_gather x1, waiting for transfers between devices, shards(): lax.all_gather(up_weight, 'cand', axis=0, tiled=True)  31.8 us
    all_gather x1, waiting for transfers between devices, shards(): lax.all_gather(gate_weight, 'cand', axis=0, tiled=True)  22.5 us
  transfers between devices with their start and end apart: 11, of which 10 were waited for; matrix products, arithmetic and copies ran while one was open for 10% of the time, Pallas kernels for 0%

profile of v1, /device:TPU:0, one launch (start us, length us, event | category | flops | bytes accessed | tf_op | source)
XLA Modules:
  0.0 386.9 jit_solution(14244680704641964696)
XLA Ops:
  10.0 14.6 %collective-permute-done = bf16[1024,512]{1,0:T(8,128)(2,1)S(1)} collective-permute-done((bf16[1024,512]{1,0:T(8,128)(2,1)}, bf16[1024,512]{1,0:T(8,128)(2,1)S(1)}, u32[]{:S(2)}, u32[]{:S(2)}) %collective-permute-start) | collective-permute-done | bytes 1048608 | tf_op jit(solution)/shard_map/ppermute | solution.py:16
  24.7 14.2 %collective-permute-done.1 = bf16[1024,512]{1,0:T(8,128)(2,1)S(1)} collective-permute-done((bf16[1024,512]{1,0:T(8,128)(2,1)S(1)}, bf16[1024,512]{1,0:T(8,128)(2,1)S(1)}, u32[]{:S(2)}, u32[]{:S(2)}) %collective-permute-start.1) | collective-permute-done | bytes 1048608 | tf_op jit(solution)/shard_map/ppermute | solution.py:16
  39.6 1.3 fusion.18
  41.5 11.6 %collective-permute-done.2 = bf16[1024,512]{1,0:T(8,128)(2,1)} collective-permute-done((bf16[1024,512]{1,0:T(8,128)(2,1)S(1)}, bf16[1024,512]{1,0:T(8,128)(2,1)}, u32[]{:S(2)}, u32[]{:S(2)}) %collective-permute-start.2) | collective-permute-done | bytes 1048608 | tf_op jit(solution)/shard_map/ppermute | solution.py:16
  53.2 2.3 constant_dynamic-update-slice_fusion.7
  55.5 1.2 constant_dynamic-update-slice_fusion.6
  56.7 1.1 constant_dynamic-update-slice_fusion.5
  57.8 1.1 constant_dynamic-update-slice_fusion.4
  58.9 2.4 constant_dynamic-update-slice_fusion.3
  61.3 1.1 constant_dynamic-update-slice_fusion.2
  62.5 1.1 constant_dynamic-update-slice_fusion.1
  63.6 1.1 constant_dynamic-update-slice_fusion
  64.7 22.5 %all-gather.11.cloned.1.call-done = bf16[2048,1024]{1,0:T(8,128)(2,1)} async-done(((bf16[512,1024]{1,0:T(8,128)(2,1)}), bf16[2048,1024]{1,0:T(8,128)(2,1)}) %all-gather.11.cloned.1.call-update) | async-done | bytes 4194320 | tf_op jit(solution)/shard_map/all_gather | solution.py:34
  87.2 4.2 %fusion.12 = f32[256,1024]{0,1:T(8,128)S(1)} fusion(bf16[2048,1024]{1,0:T(8,128)(2,1)} %all-gather.11.cloned.1.call-done, bf16[1,256,2048]{2,1,0:T(8,128)(2,1)} %all-gather.7.cloned.1.call-done), kind=kOutput, calls=%fused_computation.12 | convolution fusion | flops 1073741824 | bytes 6291456 | tf_op jit(solution)/shard_map/dot_general | solution.py:43
  91.5 31.8 %all-gather.9.cloned.1.call-done = bf16[2048,1024]{1,0:T(8,128)(2,1)} async-done(((bf16[512,1024]{1,0:T(8,128)(2,1)}), bf16[2048,1024]{1,0:T(8,128)(2,1)}) %all-gather.9.cloned.1.call-update) | async-done | bytes 4194320 | tf_op jit(solution)/shard_map/all_gather | solution.py:35
  123.3 4.9 %fusion.14 = f32[256,1024]{0,1:T(8,128)} fusion(bf16[2048,1024]{1,0:T(8,128)(2,1)} %all-gather.9.cloned.1.call-done, bf16[1,256,2048]{2,1,0:T(8,128)(2,1)S(1)} %copy-done.1), kind=kOutput, calls=%fused_computation.14 | convolution fusion | flops 1073741824 | bytes 6291456 | tf_op jit(solution)/shard_map/dot_general | solution.py:44
  128.2 36.4 %all-gather.5.cloned.1.call-done = bf16[1,256,2048]{2,1,0:T(8,128)(2,1)} async-done(((bf16[1,256,256]{2,1,0:T(8,128)(2,1)}), bf16[1,256,2048]{2,1,0:T(8,128)(2,1)}) %all-gather.5.cloned.1.call-update) | async-done | bytes 1048592 | tf_op jit(solution)/shard_map/all_gather | solution.py:29
  164.6 4.5 %multiply_convert_fusion.1 = (bf16[256,1024]{0,1:T(8,128)(2,1)S(1)}, bf16[256,1024]{0,1:T(8,128)(2,1)S(1)}) fusion(f32[256,1024]{0,1:T(8,128)S(1)} %fusion.12, f32[]{:T(128)S(6)} %convert_element_type.45, f32[256,1024]{0,1:T(8,128)} %fusion.14, bf16[1,256,2048]{2,1,0:T(8,128)(2,1)} %all-gather.5.cloned.1.call-done, ...), kind=kOutput, calls=%fused_computation.19 | convolution fusion | flops 1077936128 | bytes 8390144 | tf_op jit(solution)/shard_map/td,fd->tf/dot_general | solution.py:48
  169.2 1.3 fusion.21
  171.3 2.3 fusion.3
  173.7 3.2 convert_bitcast_fusion.1
  177.0 3.2 convert_bitcast_fusion
  180.3 1.1 copy-done.6
  181.5 4.5 %convolution_convert_fusion = bf16[1024,2048]{1,0:T(8,128)(2,1)} fusion(bf16[1,256,2048]{2,1,0:T(8,128)(2,1)S(1)} %copy-done.4, f32[256,1024]{0,1:T(8,128)} %fusion.14, f32[256,1024]{0,1:T(8,128)S(1)} %copy-done.6, f32[]{:T(128)S(6)} %convert_element_type.45), kind=kOutput, calls=%fused_computation.4 | convolution fusion | flops 1077673984 | bytes 7340036 | tf_op jit(solution)/shard_map/tf,td->fd/dot_general | solution.py:51
  186.0 51.4 %reduce-scatter.5.cloned.1.call-done = bf16[1,256,256]{2,1,0:T(8,128)(2,1)} async-done(((bf16[1,256,2048]{2,1,0:T(8,128)(2,1)}), bf16[1,256,256]{2,1,0:T(8,128)(2,1)}) %reduce-scatter.5.cloned.1.call-update) | async-done | bytes 131088 | tf_op jit(solution)/shard_map/reduce_scatter | solution.py:60
  237.4 1.6 convert_element_type.50
  239.0 44.2 %reduce-scatter.7.cloned.1.call-done = bf16[512,1024]{0,1:T(8,128)(2,1)} async-done(((bf16[2048,1024]{0,1:T(8,128)(2,1)}), bf16[512,1024]{0,1:T(8,128)(2,1)}) %reduce-scatter.7.cloned.1.call-update) | async-done | bytes 1048592 | tf_op jit(solution)/shard_map/reduce_scatter | solution.py:64
  283.3 2.6 copy.16
  285.8 44.4 %reduce-scatter.9.cloned.1.call-done = bf16[512,1024]{0,1:T(8,128)(2,1)} async-done(((bf16[2048,1024]{0,1:T(8,128)(2,1)}), bf16[512,1024]{0,1:T(8,128)(2,1)}) %reduce-scatter.9.cloned.1.call-update) | async-done | bytes 1048592 | tf_op jit(solution)/shard_map/reduce_scatter | solution.py:67
  330.2 2.6 copy.17
  332.8 44.4 %reduce-scatter.11.cloned.1.call-done = bf16[1024,512]{1,0:T(8,128)(2,1)} async-done(((bf16[1024,2048]{1,0:T(8,128)(2,1)}), bf16[1024,512]{1,0:T(8,128)(2,1)}) %reduce-scatter.11.cloned.1.call-update) | async-done | bytes 1048592 | tf_op jit(solution)/shard_map/reduce_scatter | solution.py:71
  377.2 2.8 convert_element_type.59
  (33 shorter events, 3.9 us)
Async XLA Ops:
  7.2 57.6 %all-gather.7.cloned.1.call-start = ((), (), s32[]{:S(2)}) async-start(), calls=%async_computation.5 | async-start | bytes 1179648 | tf_op jit(solution)/shard_map/all_gather | solution.py:28
  7.9 49.9 %copy-start = (bf16[1024,512]{1,0:T(8,128)(2,1)S(1)}, bf16[1024,512]{1,0:T(8,128)(2,1)}, u32[]{:S(2)}) copy-start(bf16[1024,512]{1,0:T(8,128)(2,1)} %param.11) | copy-start | bytes 3145732
  7.9 79.3 %all-gather.11.cloned.1.call-start = ((), (), s32[]{:S(2)}) async-start(), calls=%async_computation.7 | async-start | bytes 5242880 | tf_op jit(solution)/shard_map/all_gather | solution.py:34
  8.7 114.6 %all-gather.9.cloned.1.call-start = ((), (), s32[]{:S(2)}) async-start(), calls=%async_computation.6 | async-start | bytes 5242880 | tf_op jit(solution)/shard_map/all_gather | solution.py:35
  9.4 155.2 %all-gather.5.cloned.1.call-start = ((), (), s32[]{:S(2)}) async-start(), calls=%async_computation.4 | async-start | bytes 1179648 | tf_op jit(solution)/shard_map/all_gather | solution.py:29
  9.4 15.2 %collective-permute-start = (bf16[1024,512]{1,0:T(8,128)(2,1)}, bf16[1024,512]{1,0:T(8,128)(2,1)S(1)}, u32[]{:S(2)}, u32[]{:S(2)}) collective-permute-start(bf16[1024,512]{1,0:T(8,128)(2,1)} %param.11), channel_id=1, source_target_pairs={{0,8},{8,16},{16,24},{24,0},{1,9},{9,17},{17,25},{25,1},{2,10},{10... | collective-permute-start | bytes 3145736 | tf_op jit(solution)/shard_map/ppermute | solution.py:16
  24.6 14.2 %collective-permute-start.1 = (bf16[1024,512]{1,0:T(8,128)(2,1)S(1)}, bf16[1024,512]{1,0:T(8,128)(2,1)S(1)}, u32[]{:S(2)}, u32[]{:S(2)}) collective-permute-start(bf16[1024,512]{1,0:T(8,128)(2,1)S(1)} %collective-permute-done), channel_id=1, source_target_pairs={{0,8},{8,16},{16,24},{24,0},{1,9},{9,17},{17,25},{25,1},{2,10},{10... | collective-permute-start | bytes 3145736 | tf_op jit(solution)/shard_map/ppermute | solution.py:16
  38.8 14.3 %collective-permute-start.2 = (bf16[1024,512]{1,0:T(8,128)(2,1)S(1)}, bf16[1024,512]{1,0:T(8,128)(2,1)}, u32[]{:S(2)}, u32[]{:S(2)}) collective-permute-start(bf16[1024,512]{1,0:T(8,128)(2,1)S(1)} %collective-permute-done.1), channel_id=1, source_target_pairs={{0,8},{8,16},{16,24},{24,0},{1,9},{9,17},{17,25},{25,1},{2,10},{10... | collective-permute-start | bytes 3145736 | tf_op jit(solution)/shard_map/ppermute | solution.py:16
  38.9 198.5 %reduce-scatter.5.cloned.1.call-start = ((), (), s32[]{:S(2)}) async-start(), calls=%async_computation.8 | async-start | bytes 1179648 | tf_op jit(solution)/shard_map/reduce_scatter | solution.py:60
  64.7 58.6 %copy-start.1 = (bf16[1,256,2048]{2,1,0:T(8,128)(2,1)S(1)}, bf16[1,256,2048]{2,1,0:T(8,128)(2,1)}, u32[]{:S(2)}) copy-start(bf16[1,256,2048]{2,1,0:T(8,128)(2,1)} %all-gather.7.cloned.1.call-done) | copy-start | bytes 3145732
  91.5 77.6 %copy-start.5 = (f32[256,1024]{0,1:T(8,128)}, f32[256,1024]{0,1:T(8,128)S(1)}, u32[]{:S(2)}) copy-start(f32[256,1024]{0,1:T(8,128)S(1)} %fusion.12) | copy-start | bytes 3145732
  164.6 4.5 %copy-start.2 = (bf16[2048,1024]{1,0:T(8,128)(2,1)S(1)}, bf16[2048,1024]{1,0:T(8,128)(2,1)}, u32[]{:S(2)}) copy-start(bf16[2048,1024]{1,0:T(8,128)(2,1)} %all-gather.11.cloned.1.call-done) | copy-start | bytes 12582916
  169.1 2.2 copy-start.3
  173.7 109.6 %reduce-scatter.7.cloned.1.call-start = ((), (), s32[]{:S(2)}) async-start(), calls=%async_computation.9 | async-start | bytes 5242880 | tf_op jit(solution)/shard_map/reduce_scatter | solution.py:64
  176.9 3.4 copy-start.4
  177.0 153.3 %reduce-scatter.9.cloned.1.call-start = ((), (), s32[]{:S(2)}) async-start(), calls=%async_computation.10 | async-start | bytes 5242880 | tf_op jit(solution)/shard_map/reduce_scatter | solution.py:67
  180.2 1.2 copy-start.6
  180.3 196.9 %reduce-scatter.11.cloned.1.call-start = ((), (), s32[]{:S(2)}) async-start(), calls=%async_computation.11 | async-start | bytes 5242880 | tf_op jit(solution)/shard_map/reduce_scatter | solution.py:71
Sparse Core Ops, SparseCore 0:
  10.0 42.1 all-gather.6
  53.7 33.4 all-gather.10
  88.8 34.4 all-gather.8
  125.2 39.3 all-gather.4
  173.8 63.5 reduce-scatter.4
  239.8 43.4 reduce-scatter.6
  285.8 44.3 reduce-scatter.8
  332.8 44.3 reduce-scatter.10
